TPU v7x, 32 devices: a whole 2x2x4 slice. The times are simulated.
32 devices in a mesh: parts: 2 (over y), seq: 4 (over z), head: 2 (over x), fsdp: 2 (over core).
Axes of the slice: x: 2, y: 2, z: 4, core: 2. Of those that a mesh axis runs over, the one named last changes fastest.
Arguments:
- frames: bfloat16 [2048, 1024], P(('parts', 'seq', 'head', 'fsdp')), parts along dimension 0, may hold values from -24 to 24
- length: int32 [2], P('parts'), parts along dimension 0, may hold values from 512 to 1024
- ln1_gain: float32 [1024], replicated, may hold values from 0.1 to 1.9
- w_query: bfloat16 [1024, 1024], P('seq', ('head', 'fsdp')), may hold values from -0.2 to 0.2
- w_key: bfloat16 [1024, 1024], P('seq', ('head', 'fsdp')), may hold values from -3 to 3
- w_value: bfloat16 [1024, 1024], P('seq', ('head', 'fsdp')), may hold values from -0.375 to 0.375
- w_out: bfloat16 [1024, 1024], P(('head', 'fsdp'), 'seq'), may hold values from -0.1875 to 0.1875
- ln2_gain: float32 [1024], replicated, may hold values from 0.1 to 1.9
- pw1_value: bfloat16 [1024, 1024], P('seq', ('head', 'fsdp')), may hold values from -0.1875 to 0.1875
- pw1_gate: bfloat16 [1024, 1024], P('seq', ('head', 'fsdp')), may hold values from -0.375 to 0.375
- depth_kernel: float32 [9, 1024], P(None, ('head', 'fsdp')), may hold values from -2 to 2
- bn_scale: float32 [1024], P(('head', 'fsdp')), may hold values from 0.1 to 1.9
- bn_shift: float32 [1024], P(('head', 'fsdp')), may hold values from -3 to 3
- pw2: bfloat16 [1024, 1024], P(('head', 'fsdp'), 'seq'), may hold values from -0.1875 to 0.1875
Outputs:
- encoded: bfloat16 [2048, 1024], P(('parts', 'seq', 'head', 'fsdp')), parts along dimension 0
There are 2 independent parts, one for each index of `parts`. A program takes and returns all parts, laid end to end along the dimension named above; an argument that names none is the same for every part. Nothing has to cross between parts.
All inputs are finite; a program needn't handle non-finite values.
Results may differ from a plain program's by a relative error of at most 0.012.
The roundings to bfloat16 on the way count: a program that leaves them out, or rounds other values in their place, can miss the bound.
Values may be sent and summed in bfloat16 or wider, within the bound.
No kernel may reach another device: no remote copies, remote signals or barrier semaphores. Data moves between devices by JAX's collectives and lax.ppermute only.
A program may use at most 64 MiB of HBM per device.

v0:
```python
import math
import jax
import jax.numpy as jnp
from jax import lax
from jax.sharding import PartitionSpec as P

KERNEL = 9
HD = 128


def with_halo(block, sides, width):
    for axis, dim in sides:
        count = lax.axis_size(axis)
        forward = [(i, i + 1) for i in range(count - 1)]
        backward = [(target, source) for source, target in forward]
        low = lax.ppermute(
            lax.slice_in_dim(block, block.shape[dim] - width, None, axis=dim), axis, forward
        )
        high = lax.ppermute(lax.slice_in_dim(block, 0, width, axis=dim), axis, backward)
        block = jnp.concatenate([low, block, high], axis=dim)
    return block


def layer_norm(values_in, gain_vec):
    center = jnp.mean(values_in, axis=-1, keepdims=True)
    shifted = values_in - center
    spread = jnp.mean(shifted * shifted, axis=-1, keepdims=True)
    return shifted * lax.rsqrt(spread + 1e-05) * gain_vec


def shards(
    frames,
    length,
    ln1_gain,
    w_query,
    w_key,
    w_value,
    w_out,
    ln2_gain,
    pw1_value,
    pw1_gate,
    depth_kernel,
    bn_scale,
    bn_shift,
    pw2,
):
    group_size = lax.axis_size(("head", "fsdp"))
    my_rows = frames.shape[0]
    block_rows = my_rows * group_size
    head_cols = w_query.shape[1]
    heads_here = head_cols // HD
    seq_start = lax.axis_index("seq") * block_rows
    valid_len = length[0]
    score_scale = 1.0 / math.sqrt(HD)
    full_query, full_key, full_value, value_cols, gate_cols = (
        lax.all_gather(w_query, "seq", axis=0, tiled=True),
        lax.all_gather(w_key, "seq", axis=0, tiled=True),
        lax.all_gather(w_value, "seq", axis=0, tiled=True),
        lax.all_gather(pw1_value, "seq", axis=0, tiled=True),
        lax.all_gather(pw1_gate, "seq", axis=0, tiled=True),
    )
    out_rows, down_rows = (
        lax.all_gather(w_out, "seq", axis=1, tiled=True),
        lax.all_gather(pw2, "seq", axis=1, tiled=True),
    )
    projector = jnp.concatenate((full_query, full_key, full_value), axis=1)
    source = frames.astype(jnp.float32)
    normed = layer_norm(source, ln1_gain).astype(jnp.bfloat16)
    projected = jnp.dot(
        lax.all_gather(normed, ("head", "fsdp"), axis=0, tiled=True),
        projector,
        preferred_element_type=jnp.float32,
    ).astype(jnp.bfloat16)
    queries = projected[:, :head_cols].reshape(block_rows, heads_here, HD)
    keys_here = projected[:, head_cols : 2 * head_cols]
    values_here = projected[:, 2 * head_cols :]
    initial = (
        jnp.full((heads_here, block_rows), -1e30, jnp.float32),
        jnp.zeros((heads_here, block_rows), jnp.float32),
        jnp.zeros((heads_here, block_rows, HD), jnp.float32),
    )
    key_piece = lax.all_gather(keys_here, "seq", axis=0, tiled=True)
    value_piece = lax.all_gather(values_here, "seq", axis=0, tiled=True)
    row_count = key_piece.shape[0]
    block_size = math.gcd(row_count, 512)
    block_count = row_count // block_size
    key_blocks = key_piece.reshape(block_count, block_size, heads_here, HD)
    value_blocks = value_piece.reshape(block_count, block_size, heads_here, HD)
    places = jnp.arange(row_count, dtype=jnp.int32).reshape(block_count, block_size)

    def advance(inner_state, block_item):
        key_block, value_block, place = block_item
        peak_score, weight_sum, weighted = inner_state
        scores = (
            jnp.einsum("qhd,khd->hqk", queries, key_block, preferred_element_type=jnp.float32)
            * score_scale
        )
        scores = jnp.where((place < valid_len)[None, None, :], scores, -jnp.inf)
        new_peak = jnp.maximum(peak_score, jnp.max(scores, axis=2))
        factor = jnp.exp(peak_score - new_peak)
        weights = jnp.exp(scores - new_peak[:, :, None])
        weight_sum = weight_sum * factor + jnp.sum(weights, axis=2)
        weighted = weighted * factor[:, :, None] + jnp.einsum(
            "hqk,khd->hqd",
            weights.astype(jnp.bfloat16),
            value_block,
            preferred_element_type=jnp.float32,
        )
        return ((new_peak, weight_sum, weighted), None)

    result, unused = lax.scan(advance, initial, (key_blocks, value_blocks, places))
    peak_score, weight_sum, weighted = result
    context = (
        (weighted / weight_sum[:, :, None])
        .astype(jnp.bfloat16)
        .transpose(1, 0, 2)
        .reshape(block_rows, head_cols)
    )
    attended = lax.psum_scatter(
        jnp.dot(context, out_rows, preferred_element_type=jnp.float32).astype(jnp.bfloat16),
        ("head", "fsdp"),
        scatter_dimension=0,
        tiled=True,
    ).astype(jnp.float32)
    middle = source + attended
    normed_two = layer_norm(middle, ln2_gain).astype(jnp.bfloat16)
    piece = lax.all_gather(normed_two, ("head", "fsdp"), axis=0, tiled=True)
    value_part = jnp.dot(piece, value_cols, preferred_element_type=jnp.float32)
    gate_part = jnp.dot(piece, gate_cols, preferred_element_type=jnp.float32)
    places = seq_start + jnp.arange(piece.shape[0], dtype=jnp.int32)
    gated_rows = jnp.where(
        (places < valid_len)[:, None], value_part * jax.nn.sigmoid(gate_part), 0.0
    ).astype(jnp.bfloat16)
    rim_width = (KERNEL - 1) // 2
    padded = with_halo(gated_rows, (("seq", 0),), rim_width).astype(jnp.float32)
    depth_sum = depth_kernel[0] * padded[0:block_rows]
    for offset in range(1, KERNEL):
        depth_sum = depth_sum + depth_kernel[offset] * padded[offset : offset + block_rows]
    shifted = depth_sum * bn_scale + bn_shift
    active = (shifted * jax.nn.sigmoid(shifted)).astype(jnp.bfloat16)
    conv_part = lax.psum_scatter(
        jnp.dot(active, down_rows, preferred_element_type=jnp.float32).astype(jnp.bfloat16),
        ("head", "fsdp"),
        scatter_dimension=0,
        tiled=True,
    ).astype(jnp.float32)
    return (middle + conv_part).astype(jnp.bfloat16)


def solution(mesh):
    in_specs = (
        P(("parts", "seq", "head", "fsdp"), None),
        P("parts"),
        P(),
        P("seq", ("head", "fsdp")),
        P("seq", ("head", "fsdp")),
        P("seq", ("head", "fsdp")),
        P(("head", "fsdp"), "seq"),
        P(),
        P("seq", ("head", "fsdp")),
        P("seq", ("head", "fsdp")),
        P(None, ("head", "fsdp")),
        P(("head", "fsdp")),
        P(("head", "fsdp")),
        P(("head", "fsdp"), "seq"),
    )
    out_specs = P(("parts", "seq", "head", "fsdp"), None)
    return jax.shard_map(shards, mesh=mesh, in_specs=in_specs, out_specs=out_specs, check_vma=False)
```

profile of v0, /device:TPU:0, one launch (start us, length us, event | category | flops | bytes accessed | tf_op | source)
XLA Modules:
  0.0 217.0 jit_solution(8973462292048037482)
XLA Ops:
  6.6 1.1 convert_reduce_fusion
  7.7 1.1 fusion.24
  8.8 1.0 fusion.26
  9.8 8.8 %all_gather.33 = bf16[256,1024]{1,0:T(8,128)(2,1)S(1)} all-gather(bf16[64,1024]{1,0:T(8,128)(2,1)S(1)} %fusion.26), channel_id=1, replica_groups=mesh['parts'=2,'seq'=4,'head'=2,'fsdp'=2] {'head','fsdp'}, dimensions={0}, use_global_device_ids=true | all-gather | bytes 655360 | tf_op jit(solution)/shard_map/all_gather | solution.py:70
  18.6 16.3 %all_gather.34 = bf16[1024,256]{1,0:T(8,128)(2,1)S(1)} all-gather(bf16[256,256]{1,0:T(8,128)(2,1)S(1)} %copy-done.2), channel_id=1, replica_groups=mesh['parts'=2,'seq'=4,'head'=2,'fsdp'=2] {'seq'}, dimensions={0}, use_global_device_ids=true | all-gather | bytes 655360 | tf_op jit(solution)/shard_map/all_gather | solution.py:56
  34.9 15.9 %all_gather.35 = bf16[1024,256]{1,0:T(8,128)(2,1)S(1)} all-gather(bf16[256,256]{1,0:T(8,128)(2,1)S(1)} %copy-done.3), channel_id=1, replica_groups=mesh['parts'=2,'seq'=4,'head'=2,'fsdp'=2] {'seq'}, dimensions={0}, use_global_device_ids=true | all-gather | bytes 655360 | tf_op jit(solution)/shard_map/all_gather | solution.py:57
  50.8 16.1 %all_gather.36 = bf16[1024,256]{1,0:T(8,128)(2,1)S(1)} all-gather(bf16[256,256]{1,0:T(8,128)(2,1)S(1)} %copy-done.4), channel_id=1, replica_groups=mesh['parts'=2,'seq'=4,'head'=2,'fsdp'=2] {'seq'}, dimensions={0}, use_global_device_ids=true | all-gather | bytes 655360 | tf_op jit(solution)/shard_map/all_gather | solution.py:58
  67.6 14.8 %all_gather.37 = bf16[1024,256]{1,0:T(8,128)(2,1)S(1)} all-gather(bf16[256,256]{1,0:T(8,128)(2,1)S(1)} %get-tuple-element.129), channel_id=1, replica_groups=mesh['parts'=2,'seq'=4,'head'=2,'fsdp'=2] {'seq'}, dimensions={0}, use_global_device_ids=true | all-gather | bytes 655360 | tf_op jit(solution)/shard_map/all_gather | solution.py:82
  82.5 16.1 %all_gather.38 = bf16[1024,256]{1,0:T(8,128)(2,1)S(1)} all-gather(bf16[256,256]{1,0:T(8,128)(2,1)S(1)} %get-tuple-element.127), channel_id=1, replica_groups=mesh['parts'=2,'seq'=4,'head'=2,'fsdp'=2] {'seq'}, dimensions={0}, use_global_device_ids=true | all-gather | bytes 655360 | tf_op jit(solution)/shard_map/all_gather | solution.py:83
  98.8 4.0 %while.15 = (s32[]{:T(128)}, f32[2,256]{1,0:T(2,128)S(1)}, f32[2,256]{1,0:T(2,128)S(1)}, f32[2,256,128]{2,1,0:T(8,128)S(1)}, s32[2,512]{1,0:T(2,128)S(1)}, /*ind...) while((s32[]{:T(128)}, f32[2,256]{1,0:T(2,128)S(1)}, ...), condition=%wide.region_5.6_spmd.clone, body=%wide.region_2.5_spmd.clone.sunk | while | flops 136252416 | bytes 5409925 | solution.py:111
  103.0 15.8 %all_gather.39 = bf16[256,1024]{1,0:T(8,128)(2,1)S(1)} all-gather(bf16[256,256]{1,0:T(8,128)(2,1)S(1)} %copy-done.5), channel_id=1, replica_groups=mesh['parts'=2,'seq'=4,'head'=2,'fsdp'=2] {'seq'}, dimensions={1}, use_global_device_ids=true | all-gather | bytes 655360 | tf_op jit(solution)/shard_map/all_gather | solution.py:63
  118.8 1.1 convolution_convert_fusion.1
  120.7 15.6 %all_gather.42 = bf16[1024,256]{1,0:T(8,128)(2,1)S(1)} all-gather(bf16[256,256]{1,0:T(8,128)(2,1)S(1)} %copy-done.6), channel_id=1, replica_groups=mesh['parts'=2,'seq'=4,'head'=2,'fsdp'=2] {'seq'}, dimensions={0}, use_global_device_ids=true | all-gather | bytes 655360 | tf_op jit(solution)/shard_map/all_gather | solution.py:60
  136.2 15.0 %all_gather.41 = bf16[1024,256]{1,0:T(8,128)(2,1)S(1)} all-gather(bf16[256,256]{1,0:T(8,128)(2,1)S(1)} %copy-done.7), channel_id=1, replica_groups=mesh['parts'=2,'seq'=4,'head'=2,'fsdp'=2] {'seq'}, dimensions={0}, use_global_device_ids=true | all-gather | bytes 655360 | tf_op jit(solution)/shard_map/all_gather | solution.py:59
  151.3 1.0 fusion.37
  152.3 1.1 multiply_reduce_fusion
  153.5 1.0 multiply_convert_fusion.1
  154.5 6.8 %all_gather.40 = bf16[256,1024]{1,0:T(8,128)(2,1)S(1)} all-gather(bf16[64,1024]{1,0:T(8,128)(2,1)S(1)} %multiply_convert_fusion.1), channel_id=1, replica_groups=mesh['parts'=2,'seq'=4,'head'=2,'fsdp'=2] {'head','fsdp'}, dimensions={0}, use_global_device_ids=true | all-gather | bytes 655360 | tf_op jit(solution)/shard_map/all_gather | solution.py:127
  161.9 3.9 %collective-permute-start = (bf16[4,256]{1,0:T(4,128)(2,1)S(1)}, bf16[4,256]{1,0:T(4,128)(2,1)S(1)}, u32[]{:S(2)}, u32[]{:S(2)}) collective-permute-start(bf16[4,256]{1,0:T(4,128)(2,1)S(1)} %get-tuple-element.130), channel_id=1, source_target_pairs={{0,4},{4,8},{8,12},{1,5},{5,9},{9,13},{2,6},{6,10},{10,14},{3,7},{... | collective-permute-start | bytes 6152 | tf_op jit(solution)/shard_map/ppermute | solution.py:16
  165.8 1.3 collective-permute-start.1
  167.2 16.9 %all_gather.43 = bf16[256,1024]{1,0:T(8,128)(2,1)S(1)} all-gather(bf16[256,256]{1,0:T(8,128)(2,1)S(1)} %copy-done.8), channel_id=1, replica_groups=mesh['parts'=2,'seq'=4,'head'=2,'fsdp'=2] {'seq'}, dimensions={1}, use_global_device_ids=true | all-gather | bytes 655360 | tf_op jit(solution)/shard_map/all_gather | solution.py:64
  184.2 1.4 convolution_convert_fusion
  185.5 23.0 %reduce-scatter.5.cloned.1.call-done = bf16[64,1024]{1,0:T(8,128)(2,1)} async-done(((bf16[256,1024]{1,0:T(8,128)(2,1)}), bf16[64,1024]{1,0:T(8,128)(2,1)}) %reduce-scatter.5.cloned.1.call-update) | async-done | bytes 131088 | tf_op jit(solution)/shard_map/reduce_scatter | solution.py:141
  208.5 1.6 add_convert_fusion
  (70 shorter events, 5.8 us)
Async XLA Ops:
  6.5 12.0 %copy-start.2 = (bf16[256,256]{1,0:T(8,128)(2,1)S(1)}, bf16[256,256]{1,0:T(8,128)(2,1)}, u32[]{:S(2)}) copy-start(bf16[256,256]{1,0:T(8,128)(2,1)} %param.19) | copy-start | bytes 393220
  6.5 28.4 %copy-start.3 = (bf16[256,256]{1,0:T(8,128)(2,1)S(1)}, bf16[256,256]{1,0:T(8,128)(2,1)}, u32[]{:S(2)}) copy-start(bf16[256,256]{1,0:T(8,128)(2,1)} %param.20) | copy-start | bytes 393220
  6.5 144.7 %reduce-scatter.3.cloned.1.call-start = ((), (), s32[]{:S(2)}) async-start(), calls=%async_computation.2 | async-start | bytes 655360 | tf_op jit(solution)/shard_map/reduce_scatter | solution.py:119
  9.8 41.0 %copy-start.4 = (bf16[256,256]{1,0:T(8,128)(2,1)S(1)}, bf16[256,256]{1,0:T(8,128)(2,1)}, u32[]{:S(2)}) copy-start(bf16[256,256]{1,0:T(8,128)(2,1)} %param.21) | copy-start | bytes 393220
  98.7 4.2 %copy-start.5 = (bf16[256,256]{1,0:T(8,128)(2,1)S(1)}, bf16[256,256]{1,0:T(8,128)(2,1)}, u32[]{:S(2)}) copy-start(bf16[256,256]{1,0:T(8,128)(2,1)} %param.22) | copy-start | bytes 393220
  118.8 1.9 copy-start.6
  118.8 17.4 %copy-start.7 = (bf16[256,256]{1,0:T(8,128)(2,1)S(1)}, bf16[256,256]{1,0:T(8,128)(2,1)}, u32[]{:S(2)}) copy-start(bf16[256,256]{1,0:T(8,128)(2,1)} %param.24) | copy-start | bytes 393220
  119.9 31.3 %copy-start.9 = (f32[9,256]{1,0:T(8,128)S(1)}, f32[9,256]{1,0:T(8,128)}, u32[]{:S(2)}) copy-start(f32[9,256]{1,0:T(8,128)} %param.26) | copy-start | bytes 27652
  119.9 31.3 %copy-start = (bf16[64,1024]{1,0:T(8,128)(2,1)S(1)}, bf16[64,1024]{1,0:T(8,128)(2,1)}, u32[]{:S(2)}) copy-start(bf16[64,1024]{1,0:T(8,128)(2,1)} %param.16) | copy-start | bytes 393220
  120.0 33.5 %copy-start.10 = (f32[1024]{0:T(1024)S(1)}, f32[1024]{0:T(1024)}, u32[]{:S(2)}) copy-start(f32[1024]{0:T(1024)} %param.23) | copy-start | bytes 12292
  120.0 88.6 %reduce-scatter.5.cloned.1.call-start = ((), (), s32[]{:S(2)}) async-start(), calls=%async_computation.3 | async-start | bytes 655360 | tf_op jit(solution)/shard_map/reduce_scatter | solution.py:141
  161.6 5.6 %copy-start.8 = (bf16[256,256]{1,0:T(8,128)(2,1)S(1)}, bf16[256,256]{1,0:T(8,128)(2,1)}, u32[]{:S(2)}) copy-start(bf16[256,256]{1,0:T(8,128)(2,1)} %param.29) | copy-start | bytes 393220
  161.6 22.5 %copy-start.11 = (f32[256]{0:T(256)S(1)}, f32[256]{0:T(256)}, u32[]{:S(2)}) copy-start(f32[256]{0:T(256)} %param.28) | copy-start | bytes 3076
  161.6 22.5 %copy-start.12 = (f32[256]{0:T(256)S(1)}, f32[256]{0:T(256)}, u32[]{:S(2)}) copy-start(f32[256]{0:T(256)} %param.27) | copy-start | bytes 3076
  161.9 22.2 %collective-permute-start = (bf16[4,256]{1,0:T(4,128)(2,1)S(1)}, bf16[4,256]{1,0:T(4,128)(2,1)S(1)}, u32[]{:S(2)}, u32[]{:S(2)}) collective-permute-start(bf16[4,256]{1,0:T(4,128)(2,1)S(1)} %get-tuple-element.130), channel_id=1, source_target_pairs={{0,4},{4,8},{8,12},{1,5},{5,9},{9,13},{2,6},{6,10},{10,14},{3,7},{... | collective-permute-start | bytes 6152 | tf_op jit(solution)/shard_map/ppermute | solution.py:16
  165.8 18.3 %collective-permute-start.1 = (bf16[4,256]{1,0:T(4,128)(2,1)S(1)}, bf16[4,256]{1,0:T(4,128)(2,1)S(1)}, u32[]{:S(2)}, u32[]{:S(2)}) collective-permute-start(bf16[4,256]{1,0:T(4,128)(2,1)S(1)} %get-tuple-element.131), channel_id=1, source_target_pairs={{4,0},{8,4},{12,8},{5,1},{9,5},{13,9},{6,2},{10,6},{14,10},{7,3},{... | collective-permute-start | bytes 6152 | tf_op jit(solution)/shard_map/ppermute | solution.py:19
  184.2 24.4 %copy-start.1 = (bf16[64,1024]{1,0:T(8,128)(2,1)S(1)}, bf16[64,1024]{1,0:T(8,128)(2,1)}, u32[]{:S(2)}) copy-start(bf16[64,1024]{1,0:T(8,128)(2,1)} %reduce-scatter.3.cloned.1.call-done) | copy-start | bytes 393220
Sparse Core Ops, SparseCore 0:
  120.1 22.2 reduce-scatter.2
  185.7 22.8 reduce-scatter.4
where the time goes:
time: 217 us
  blocking collectives  158 us (73%)
  waiting for transfers between devices  23 us (11%)
  between operations  14.4 us (7%)
  other arithmetic  9.78 us (5%)
  starting transfers between devices  5.23 us (2%)
  matrix products  5.13 us (2%)
    reduce_scatter x1, waiting for transfers between devices, shards(): lax.psum_scatter(jnp.dot(active, down_rows, preferred_element_type=jnp.fl...  23 us
    all_gather x1, blocking collectives, shards(): lax.all_gather(pw2, 'seq', axis=1, tiled=True)  16.9 us
    all_gather x1, blocking collectives, shards(): lax.all_gather(w_query, 'seq', axis=0, tiled=True)  16.3 us
    all_gather x1, blocking collectives, shards(): lax.all_gather(w_value, 'seq', axis=0, tiled=True)  16.1 us
    all_gather x1, blocking collectives, shards(): value_piece = lax.all_gather(values_here, 'seq', axis=0, tiled=True)  16.1 us
    all_gather x1, blocking collectives, shards(): lax.all_gather(w_key, 'seq', axis=0, tiled=True)  15.9 us
    all_gather x1, blocking collectives, shards(): lax.all_gather(w_out, 'seq', axis=1, tiled=True)  15.8 us
    all_gather x1, blocking collectives, shards(): lax.all_gather(pw1_gate, 'seq', axis=0, tiled=True)  15.6 us
  transfers between devices with their start and end apart: 4, of which 1 were waited for; matrix products, arithmetic and copies ran while one was open for 0% of the time, Pallas kernels for 0%

commit v1 on v0

--- a/solution.py
+++ b/solution.py
@@ -6,6 +6,19 @@
 
 KERNEL = 9
 HD = 128
+
+
+def gather_around(array, axis, dim):
+    ways = lax.axis_size(axis)
+    up = [(d, (d + 1) % ways) for d in range(ways)]
+    down = [(d, (d - 1) % ways) for d in range(ways)]
+    earlier, later = ([array], [array])
+    for _ in range(ways // 2):
+        earlier.append(lax.ppermute(earlier[-1], axis, up))
+    for _ in range((ways - 1) // 2):
+        later.append(lax.ppermute(later[-1], axis, down))
+    line = jnp.concatenate([*earlier[::-1], *later[1:]], axis=dim)
+    return jnp.roll(line, (lax.axis_index(axis) - ways // 2) * array.shape[dim], axis=dim)
 
 
 def with_halo(block, sides, width):
@@ -55,7 +68,7 @@
     full_query, full_key, full_value, value_cols, gate_cols = (
         lax.all_gather(w_query, "seq", axis=0, tiled=True),
         lax.all_gather(w_key, "seq", axis=0, tiled=True),
-        lax.all_gather(w_value, "seq", axis=0, tiled=True),
+        gather_around(w_value, "seq", 0),
         lax.all_gather(pw1_value, "seq", axis=0, tiled=True),
         lax.all_gather(pw1_gate, "seq", axis=0, tiled=True),
     )

time: 217 us -> 204 us (0.940)
  blocking collectives: 158 us -> 142 us
  starting transfers between devices: 5.23 us -> 7.74 us
    all_gather x1 -> x0, blocking collectives: 16.1 us -> none  [shards(): lax.all_gather(w_value, 'seq', axis=0, tiled=True)]
    ppermute x0 -> x3, starting transfers between devices: none -> 5.11 us  [the longest x2 3.03 us: gather_around(): earlier.append(lax.ppermute(earlier[-1], axis, up))]
    ppermute x1, starting transfers between devices: 3.9 us -> 1.29 us  [with_halo(): lax.ppermute(lax.slice_in_dim(block, block.shape[dim] - width, None, axis...]
  transfers between devices with their start and end apart: 4 -> 7, of which waited for: 1 -> 1; matrix products, arithmetic and copies ran while one was open for 0% -> 2% of each run, Pallas kernels for 0% -> 0%
where the time goes in v1:
time: 204 us
  blocking collectives  142 us (70%)
  waiting for transfers between devices  23 us (11%)
  between operations  14.5 us (7%)
  other arithmetic  9.73 us (5%)
  starting transfers between devices  7.74 us (4%)
  matrix products  5.18 us (3%)
    reduce_scatter x1, waiting for transfers between devices, shards(): lax.psum_scatter(jnp.dot(active, down_rows, preferred_element_type=jnp.fl...  23 us
    all_gather x1, blocking collectives, shards(): lax.all_gather(w_out, 'seq', axis=1, tiled=True)  17.4 us
    all_gather x1, blocking collectives, shards(): lax.all_gather(pw2, 'seq', axis=1, tiled=True)  16.6 us
    all_gather x1, blocking collectives, shards(): lax.all_gather(w_key, 'seq', axis=0, tiled=True)  16.2 us
    all_gather x1, blocking collectives, shards(): lax.all_gather(w_query, 'seq', axis=0, tiled=True)  16.1 us
    all_gather x1, blocking collectives, shards(): value_piece = lax.all_gather(values_here, 'seq', axis=0, tiled=True)  16 us
    all_gather x1, blocking collectives, shards(): lax.all_gather(pw1_gate, 'seq', axis=0, tiled=True)  15.9 us
    all_gather x1, blocking collectives, shards(): key_piece = lax.all_gather(keys_here, 'seq', axis=0, tiled=True)  15 us
  transfers between devices with their start and end apart: 7, of which 1 were waited for; matrix products, arithmetic and copies ran while one was open for 2% of the time, Pallas kernels for 0%

profile of v1, /device:TPU:0, one launch (start us, length us, event | category | flops | bytes accessed | tf_op | source)
XLA Modules:
  0.0 203.6 jit_solution(13675703675355699211)
XLA Ops:
  6.5 3.0 %collective-permute-start = (bf16[256,256]{1,0:T(8,128)(2,1)}, bf16[256,256]{1,0:T(8,128)(2,1)S(1)}, u32[]{:S(2)}, u32[]{:S(2)}) collective-permute-start(bf16[256,256]{1,0:T(8,128)(2,1)} %param.21), channel_id=1, source_target_pairs={{0,4},{4,8},{8,12},{12,0},{1,5},{5,9},{9,13},{13,1},{2,6},{6,10},{... | collective-permute-start | bytes 393224 | tf_op jit(solution)/shard_map/ppermute | solution.py:17
  9.6 2.1 %collective-permute-start.2 = (bf16[256,256]{1,0:T(8,128)(2,1)}, bf16[256,256]{1,0:T(8,128)(2,1)S(1)}, u32[]{:S(2)}, u32[]{:S(2)}) collective-permute-start(bf16[256,256]{1,0:T(8,128)(2,1)} %param.21), channel_id=1, source_target_pairs={{0,12},{4,0},{8,4},{12,8},{1,13},{5,1},{9,5},{13,9},{2,14},{6,2},{... | collective-permute-start | bytes 393224 | tf_op jit(solution)/shard_map/ppermute | solution.py:19
  11.6 1.0 convert_reduce_fusion
  12.7 1.1 fusion.24
  13.8 1.0 fusion.26
  14.8 7.5 %all_gather.30 = bf16[256,1024]{1,0:T(8,128)(2,1)S(1)} all-gather(bf16[64,1024]{1,0:T(8,128)(2,1)S(1)} %fusion.26), channel_id=1, replica_groups=mesh['parts'=2,'seq'=4,'head'=2,'fsdp'=2] {'head','fsdp'}, dimensions={0}, use_global_device_ids=true | all-gather | bytes 655360 | tf_op jit(solution)/shard_map/all_gather | solution.py:83
  22.3 16.1 %all_gather.31 = bf16[1024,256]{1,0:T(8,128)(2,1)S(1)} all-gather(bf16[256,256]{1,0:T(8,128)(2,1)S(1)} %copy-done.3), channel_id=1, replica_groups=mesh['parts'=2,'seq'=4,'head'=2,'fsdp'=2] {'seq'}, dimensions={0}, use_global_device_ids=true | all-gather | bytes 655360 | tf_op jit(solution)/shard_map/all_gather | solution.py:69
  38.4 16.2 %all_gather.32 = bf16[1024,256]{1,0:T(8,128)(2,1)S(1)} all-gather(bf16[256,256]{1,0:T(8,128)(2,1)S(1)} %copy-done.4), channel_id=1, replica_groups=mesh['parts'=2,'seq'=4,'head'=2,'fsdp'=2] {'seq'}, dimensions={0}, use_global_device_ids=true | all-gather | bytes 655360 | tf_op jit(solution)/shard_map/all_gather | solution.py:70
  54.6 17.4 %all_gather.35 = bf16[256,1024]{1,0:T(8,128)(2,1)S(1)} all-gather(bf16[256,256]{1,0:T(8,128)(2,1)S(1)} %copy-done.5), channel_id=1, replica_groups=mesh['parts'=2,'seq'=4,'head'=2,'fsdp'=2] {'seq'}, dimensions={1}, use_global_device_ids=true | all-gather | bytes 655360 | tf_op jit(solution)/shard_map/all_gather | solution.py:76
  73.0 15.0 %all_gather.33 = bf16[1024,256]{1,0:T(8,128)(2,1)S(1)} all-gather(bf16[256,256]{1,0:T(8,128)(2,1)S(1)} %get-tuple-element.129), channel_id=1, replica_groups=mesh['parts'=2,'seq'=4,'head'=2,'fsdp'=2] {'seq'}, dimensions={0}, use_global_device_ids=true | all-gather | bytes 655360 | tf_op jit(solution)/shard_map/all_gather | solution.py:95
  88.1 16.0 %all_gather.34 = bf16[1024,256]{1,0:T(8,128)(2,1)S(1)} all-gather(bf16[256,256]{1,0:T(8,128)(2,1)S(1)} %get-tuple-element.127), channel_id=1, replica_groups=mesh['parts'=2,'seq'=4,'head'=2,'fsdp'=2] {'seq'}, dimensions={0}, use_global_device_ids=true | all-gather | bytes 655360 | tf_op jit(solution)/shard_map/all_gather | solution.py:96
  104.2 4.0 %while.15 = (s32[]{:T(128)}, f32[2,256]{1,0:T(2,128)S(1)}, f32[2,256]{1,0:T(2,128)S(1)}, f32[2,256,128]{2,1,0:T(8,128)S(1)}, s32[2,512]{1,0:T(2,128)S(1)}, /*ind...) while((s32[]{:T(128)}, f32[2,256]{1,0:T(2,128)S(1)}, ...), condition=%wide.region_5.6_spmd.clone, body=%wide.region_2.5_spmd.clone.sunk | while | flops 136252416 | bytes 5409925 | solution.py:124
  108.5 1.1 convolution_convert_fusion.1
  110.4 15.9 %all_gather.38 = bf16[1024,256]{1,0:T(8,128)(2,1)S(1)} all-gather(bf16[256,256]{1,0:T(8,128)(2,1)S(1)} %copy-done.6), channel_id=1, replica_groups=mesh['parts'=2,'seq'=4,'head'=2,'fsdp'=2] {'seq'}, dimensions={0}, use_global_device_ids=true | all-gather | bytes 655360 | tf_op jit(solution)/shard_map/all_gather | solution.py:73
  126.3 14.8 %all_gather.37 = bf16[1024,256]{1,0:T(8,128)(2,1)S(1)} all-gather(bf16[256,256]{1,0:T(8,128)(2,1)S(1)} %copy-done.7), channel_id=1, replica_groups=mesh['parts'=2,'seq'=4,'head'=2,'fsdp'=2] {'seq'}, dimensions={0}, use_global_device_ids=true | all-gather | bytes 655360 | tf_op jit(solution)/shard_map/all_gather | solution.py:72
  141.1 1.0 fusion.37
  142.2 1.1 multiply_reduce_fusion
  144.3 6.5 %all_gather.36 = bf16[256,1024]{1,0:T(8,128)(2,1)S(1)} all-gather(bf16[64,1024]{1,0:T(8,128)(2,1)S(1)} %multiply_convert_fusion.1), channel_id=1, replica_groups=mesh['parts'=2,'seq'=4,'head'=2,'fsdp'=2] {'head','fsdp'}, dimensions={0}, use_global_device_ids=true | all-gather | bytes 655360 | tf_op jit(solution)/shard_map/all_gather | solution.py:140
  151.5 1.3 collective-permute-start.3
  152.8 1.3 collective-permute-start.4
  154.1 16.6 %all_gather.39 = bf16[256,1024]{1,0:T(8,128)(2,1)S(1)} all-gather(bf16[256,256]{1,0:T(8,128)(2,1)S(1)} %copy-done.8), channel_id=1, replica_groups=mesh['parts'=2,'seq'=4,'head'=2,'fsdp'=2] {'seq'}, dimensions={1}, use_global_device_ids=true | all-gather | bytes 655360 | tf_op jit(solution)/shard_map/all_gather | solution.py:77
  170.8 1.4 convolution_convert_fusion
  172.2 23.0 %reduce-scatter.5.cloned.1.call-done = bf16[64,1024]{1,0:T(8,128)(2,1)} async-done(((bf16[256,1024]{1,0:T(8,128)(2,1)}), bf16[64,1024]{1,0:T(8,128)(2,1)}) %reduce-scatter.5.cloned.1.call-update) | async-done | bytes 131088 | tf_op jit(solution)/shard_map/reduce_scatter | solution.py:154
  195.2 1.6 add_convert_fusion
  (84 shorter events, 7.0 us)
Async XLA Ops:
  6.5 15.8 %copy-start.3 = (bf16[256,256]{1,0:T(8,128)(2,1)S(1)}, bf16[256,256]{1,0:T(8,128)(2,1)}, u32[]{:S(2)}) copy-start(bf16[256,256]{1,0:T(8,128)(2,1)} %param.19) | copy-start | bytes 393220
  6.5 31.9 %copy-start.4 = (bf16[256,256]{1,0:T(8,128)(2,1)S(1)}, bf16[256,256]{1,0:T(8,128)(2,1)}, u32[]{:S(2)}) copy-start(bf16[256,256]{1,0:T(8,128)(2,1)} %param.20) | copy-start | bytes 393220
  6.5 134.5 %reduce-scatter.3.cloned.1.call-start = ((), (), s32[]{:S(2)}) async-start(), calls=%async_computation.2 | async-start | bytes 655360 | tf_op jit(solution)/shard_map/reduce_scatter | solution.py:132
  6.5 48.1 %collective-permute-start = (bf16[256,256]{1,0:T(8,128)(2,1)}, bf16[256,256]{1,0:T(8,128)(2,1)S(1)}, u32[]{:S(2)}, u32[]{:S(2)}) collective-permute-start(bf16[256,256]{1,0:T(8,128)(2,1)} %param.21), channel_id=1, source_target_pairs={{0,4},{4,8},{8,12},{12,0},{1,5},{5,9},{9,13},{13,1},{2,6},{6,10},{... | collective-permute-start | bytes 393224 | tf_op jit(solution)/shard_map/ppermute | solution.py:17
  9.6 62.6 %collective-permute-start.2 = (bf16[256,256]{1,0:T(8,128)(2,1)}, bf16[256,256]{1,0:T(8,128)(2,1)S(1)}, u32[]{:S(2)}, u32[]{:S(2)}) collective-permute-start(bf16[256,256]{1,0:T(8,128)(2,1)} %param.21), channel_id=1, source_target_pairs={{0,12},{4,0},{8,4},{12,8},{1,13},{5,1},{9,5},{13,9},{2,14},{6,2},{... | collective-permute-start | bytes 393224 | tf_op jit(solution)/shard_map/ppermute | solution.py:19
  14.8 39.8 %copy-start.5 = (bf16[256,256]{1,0:T(8,128)(2,1)S(1)}, bf16[256,256]{1,0:T(8,128)(2,1)}, u32[]{:S(2)}) copy-start(bf16[256,256]{1,0:T(8,128)(2,1)} %param.22) | copy-start | bytes 393220
  38.4 33.7 %copy-start.2 = (bf16[256,256]{1,0:T(8,128)(2,1)S(1)}, bf16[256,256]{1,0:T(8,128)(2,1)}, u32[]{:S(2)}) copy-start(bf16[256,256]{1,0:T(8,128)(2,1)} %param.21) | copy-start | bytes 393220
  54.6 17.5 %collective-permute-start.1 = (bf16[256,256]{1,0:T(8,128)(2,1)S(1)}, bf16[256,256]{1,0:T(8,128)(2,1)S(1)}, u32[]{:S(2)}, u32[]{:S(2)}) collective-permute-start(bf16[256,256]{1,0:T(8,128)(2,1)S(1)} %collective-permute-done), channel_id=1, source_target_pairs={{0,4},{4,8},{8,12},{12,0},{1,5},{5,9},{9,13},{13,1},{2,6},{6,10},{... | collective-permute-start | bytes 393224 | tf_op jit(solution)/shard_map/ppermute | solution.py:17
  108.4 1.9 copy-start.6
  108.5 17.8 %copy-start.7 = (bf16[256,256]{1,0:T(8,128)(2,1)S(1)}, bf16[256,256]{1,0:T(8,128)(2,1)}, u32[]{:S(2)}) copy-start(bf16[256,256]{1,0:T(8,128)(2,1)} %param.24) | copy-start | bytes 393220
  109.6 31.5 %copy-start.9 = (f32[9,256]{1,0:T(8,128)S(1)}, f32[9,256]{1,0:T(8,128)}, u32[]{:S(2)}) copy-start(f32[9,256]{1,0:T(8,128)} %param.26) | copy-start | bytes 27652
  109.6 31.5 %copy-start = (bf16[64,1024]{1,0:T(8,128)(2,1)S(1)}, bf16[64,1024]{1,0:T(8,128)(2,1)}, u32[]{:S(2)}) copy-start(bf16[64,1024]{1,0:T(8,128)(2,1)} %param.16) | copy-start | bytes 393220
  109.6 33.7 %copy-start.10 = (f32[1024]{0:T(1024)S(1)}, f32[1024]{0:T(1024)}, u32[]{:S(2)}) copy-start(f32[1024]{0:T(1024)} %param.23) | copy-start | bytes 12292
  109.6 85.5 %reduce-scatter.5.cloned.1.call-start = ((), (), s32[]{:S(2)}) async-start(), calls=%async_computation.3 | async-start | bytes 655360 | tf_op jit(solution)/shard_map/reduce_scatter | solution.py:154
  151.1 3.0 %copy-start.8 = (bf16[256,256]{1,0:T(8,128)(2,1)S(1)}, bf16[256,256]{1,0:T(8,128)(2,1)}, u32[]{:S(2)}) copy-start(bf16[256,256]{1,0:T(8,128)(2,1)} %param.29) | copy-start | bytes 393220
  151.1 19.6 %copy-start.11 = (f32[256]{0:T(256)S(1)}, f32[256]{0:T(256)}, u32[]{:S(2)}) copy-start(f32[256]{0:T(256)} %param.28) | copy-start | bytes 3076
  151.2 19.6 %copy-start.12 = (f32[256]{0:T(256)S(1)}, f32[256]{0:T(256)}, u32[]{:S(2)}) copy-start(f32[256]{0:T(256)} %param.27) | copy-start | bytes 3076
  151.5 19.2 %collective-permute-start.3 = (bf16[4,256]{1,0:T(4,128)(2,1)S(1)}, bf16[4,256]{1,0:T(4,128)(2,1)S(1)}, u32[]{:S(2)}, u32[]{:S(2)}) collective-permute-start(bf16[4,256]{1,0:T(4,128)(2,1)S(1)} %get-tuple-element.130), channel_id=1, source_target_pairs={{0,4},{4,8},{8,12},{1,5},{5,9},{9,13},{2,6},{6,10},{10,14},{3,7},{... | collective-permute-start | bytes 6152 | tf_op jit(solution)/shard_map/ppermute | solution.py:29
  152.8 17.9 %collective-permute-start.4 = (bf16[4,256]{1,0:T(4,128)(2,1)S(1)}, bf16[4,256]{1,0:T(4,128)(2,1)S(1)}, u32[]{:S(2)}, u32[]{:S(2)}) collective-permute-start(bf16[4,256]{1,0:T(4,128)(2,1)S(1)} %get-tuple-element.131), channel_id=1, source_target_pairs={{4,0},{8,4},{12,8},{5,1},{9,5},{13,9},{6,2},{10,6},{14,10},{7,3},{... | collective-permute-start | bytes 6152 | tf_op jit(solution)/shard_map/ppermute | solution.py:32
  170.8 24.4 %copy-start.1 = (bf16[64,1024]{1,0:T(8,128)(2,1)S(1)}, bf16[64,1024]{1,0:T(8,128)(2,1)}, u32[]{:S(2)}) copy-start(bf16[64,1024]{1,0:T(8,128)(2,1)} %reduce-scatter.3.cloned.1.call-done) | copy-start | bytes 393220
Sparse Core Ops, SparseCore 0:
  109.7 20.2 reduce-scatter.2
  172.3 22.7 reduce-scatter.4
